TPU v7x, 256 devices: a whole 4x4x8 slice. The times are simulated.
256 devices in a mesh: row: 8 (over z_hi, core), col: 32 (over y, x, z_lo).
Axes of the slice: x: 4, y: 4, z: 8 (z_hi: 4, z_lo: 2; z = z_hi * 2 + z_lo), core: 2. Of those that a mesh axis runs over, the one named last changes fastest.
Arguments:
- tile_amps: bfloat16 [6144, 6144], P('row', 'col'), as said below
- cycle_ints: bfloat16 [6144, 6144], P('row', 'col'), as said below
- base_ints: bfloat16 [6144, 6144], P('row', 'col'), as said below
- amp_mask: int32 [96, 96], P('row', 'col'), may hold values from 0 to 1, as said below
- int_mask: int32 [96, 96], P('row', 'col'), may hold values from 0 to 1, as said below
- pair_amps: bfloat16 [64, 196608], P(None, ('row', 'col')), may hold values from -6 to 6
- ladder_ints: bfloat16 [196608, 1024], P(('row', 'col')), may hold values from -0.0546875 to 0.0546875
- pair_list: int32 [16], replicated, may hold values from 0 to 63, as said below
Outputs:
- cycle_residual: float32 [6144, 6144], P('row', 'col')
- ladder: float32 [16, 1024], P(None, 'col')
Inputs may be any that keep to these rules, and one draw needn't show every extreme that they name: `tile_amps`: equal to its transpose. `cycle_ints`: equal to its transpose. `base_ints`: equal to its transpose. `amp_mask`: 0 or 1, equal to its transpose, 1 on every diagonal tile. `int_mask`: 0 or 1, equal to its transpose, 1 on every diagonal tile. `pair_list`: distinct entries.
All inputs are finite; a program needn't handle non-finite values.
Results may differ from a plain program's by a relative error of at most 0.0029.
Values may be sent and summed in bfloat16 or wider, within the bound.
No kernel may reach another device: no remote copies, remote signals or barrier semaphores. Data moves between devices by JAX's collectives and lax.ppermute only.
A program may use at most 64 MiB of HBM per device.

v0:
```python
import jax
import jax.numpy as jnp
from jax import lax
from jax.sharding import PartitionSpec as P


def widen(mask, field):
    rows, cols = mask.shape
    tile = field.shape[0] // rows
    spread = jnp.broadcast_to(mask.astype(field.dtype)[:, None, :, None], (rows, tile, cols, tile))
    return field * spread.reshape(rows * tile, cols * tile)


def on_device(
    tile_amps, cycle_ints, base_ints, amp_mask, int_mask, pair_amps, ladder_ints, pair_list
):
    amplitudes = widen(amp_mask, tile_amps)
    integrals = widen(int_mask, cycle_ints)
    baseline = widen(int_mask, base_ints)
    amp_columns = lax.all_gather(amplitudes, "row", axis=0, tiled=True)
    section = amp_columns
    summed = baseline.astype(jnp.float32) + jnp.dot(
        lax.all_gather(integrals, "col", axis=1, tiled=True),
        section,
        preferred_element_type=jnp.float32,
    )
    intermediate = summed.astype(jnp.bfloat16)
    inter_columns = lax.all_gather(intermediate, "row", axis=0, tiled=True)
    section = inter_columns
    cycle_residual = jnp.dot(
        lax.all_gather(amplitudes, "col", axis=1, tiled=True),
        section,
        preferred_element_type=jnp.float32,
    )
    stored = pair_amps.shape[0]
    selector = (pair_list[:, None] == jnp.arange(stored, dtype=jnp.int32)[None, :]).astype(
        jnp.bfloat16
    )
    chosen = jnp.dot(selector, pair_amps, preferred_element_type=jnp.float32).astype(jnp.bfloat16)
    partial_sums = jnp.dot(chosen, ladder_ints, preferred_element_type=jnp.float32)
    totals = lax.psum(partial_sums, ("row", "col"))
    share_width = totals.shape[1] // lax.axis_size("col")
    ladder = lax.dynamic_slice_in_dim(totals, lax.axis_index("col") * share_width, share_width, 1)
    return (cycle_residual, ladder)


def solution(mesh):
    in_specs = (
        P("row", "col"),
        P("row", "col"),
        P("row", "col"),
        P("row", "col"),
        P("row", "col"),
        P(None, ("row", "col")),
        P(("row", "col"), None),
        P(),
    )
    out_specs = (P("row", "col"), P(None, "col"))
    return jax.shard_map(
        on_device, mesh=mesh, in_specs=in_specs, out_specs=out_specs, check_vma=False
    )
```

profile of v0, /device:TPU:1, one launch (start us, length us, event | category | flops | bytes accessed | tf_op | source)
XLA Modules:
  0.0 534.8 jit_solution(9945198933842615081)
XLA Ops:
  8.0 0.0 copy-start
  8.0 0.0 copy-start.3
  8.0 0.0 all-gather.9.cloned.1.call-start
  8.1 0.8 convert_element_type.17
  8.9 0.2 broadcast_in_dim.4
  9.0 0.5 reshape.14
  9.5 0.0 copy-start.2
  9.5 0.0 copy-start.4
  9.5 1.8 mul.12
  11.3 0.0 all-gather.9.cloned.1.call-update
  11.3 0.0 all-gather.7.cloned.1.call-start
  11.4 0.0 copy-done.3
  11.4 0.2 broadcast_in_dim.5
  11.6 0.0 copy-start.5
  11.6 0.5 reshape.15
  12.1 0.8 mul.14
  12.9 0.0 all-gather.7.cloned.1.call-update
  12.9 0.0 all-reduce.2.cloned.1.call-start
  13.0 1.1 fusion.1
  14.1 0.0 all-reduce.2.cloned.1.call-update
  14.1 0.0 all-gather.5.cloned.1.call-start
  14.2 0.7 all-gather.5.cloned.1.call-update
  14.9 0.0 all-gather.11.cloned.1.call-start
  14.9 39.0 %all-gather.9.cloned.1.call-done = bf16[6144,192]{0,1:T(8,128)(2,1)} async-done(((bf16[768,192]{0,1:T(8,128)(2,1)}), bf16[6144,192]{0,1:T(8,128)(2,1)}) %all-gather.9.cloned.1.call-update) | async-done | bytes 2359312 | tf_op jit(solution)/shard_map/all_gather | solution.py:20
  53.9 213.9 %all-gather.7.cloned.1.call-done = bf16[768,6144]{0,1:T(8,128)(2,1)} async-done(((bf16[768,192]{0,1:T(8,128)(2,1)}), bf16[768,6144]{0,1:T(8,128)(2,1)}) %all-gather.7.cloned.1.call-update) | async-done | bytes 9437200 | tf_op jit(solution)/shard_map/all_gather | solution.py:23
  267.8 7.1 %fusion = bf16[768,192]{0,1:T(8,128)(2,1)} fusion(bf16[6144,192]{0,1:T(8,128)(2,1)} %all-gather.9.cloned.1.call-done, bf16[768,6144]{0,1:T(8,128)(2,1)} %all-gather.7.cloned.1.call-done, bf16[768,192]{0,1:T(8,128)(2,1)S(1)} %copy-done.5, bf16[768,192]{0,1:T(8,128)(2,1)S(1)} %reshape.15), kind=kOutput, calls=%fused_computation.1 | convolution fusion | flops 1812529152 | bytes 12681216 | tf_op jit(solution)/shard_map/dot_general | solution.py:22
  274.9 0.0 all-gather.11.cloned.1.call-update
  275.0 101.3 %all-reduce.2.cloned.1.call-done = f32[16,1024]{1,0:T(8,128)} async-done(((f32[16,1024]{1,0:T(8,128)}), f32[16,1024]{1,0:T(8,128)}) %all-reduce.2.cloned.1.call-update) | async-done | bytes 65552 | tf_op jit(solution)/shard_map/psum | solution.py:41
  376.2 1.4 constant_dynamic-slice_fusion
  377.6 104.4 %all-gather.5.cloned.1.call-done = bf16[768,6144]{0,1:T(8,128)(2,1)} async-done(((bf16[768,192]{0,1:T(8,128)(2,1)}), bf16[768,6144]{0,1:T(8,128)(2,1)}) %all-gather.5.cloned.1.call-update) | async-done | bytes 9437200 | tf_op jit(solution)/shard_map/all_gather | solution.py:31
  482.0 38.5 %all-gather.11.cloned.1.call-done = bf16[6144,192]{0,1:T(8,128)(2,1)} async-done(((bf16[768,192]{0,1:T(8,128)(2,1)}), bf16[6144,192]{0,1:T(8,128)(2,1)}) %all-gather.11.cloned.1.call-update) | async-done | bytes 2359312 | tf_op jit(solution)/shard_map/all_gather | solution.py:28
  520.4 7.2 %fusion.4 = f32[768,192]{0,1:T(8,128)} fusion(bf16[6144,192]{0,1:T(8,128)(2,1)} %all-gather.11.cloned.1.call-done, bf16[768,6144]{0,1:T(8,128)(2,1)} %all-gather.5.cloned.1.call-done), kind=kOutput, calls=%fused_computation.7 | convolution fusion | flops 1811939328 | bytes 12386304 | tf_op jit(solution)/shard_map/dot_general | solution.py:30
  (7 shorter events, 0.0 us)
Async XLA Ops:
  8.0 5.0 copy-start
  8.0 3.4 copy-start.3
  8.0 45.9 %all-gather.9.cloned.1.call-start = ((), (), s32[]{:S(2)}) async-start(), calls=%async_computation.2 | async-start | bytes 2654208 | tf_op jit(solution)/shard_map/all_gather | solution.py:20
  8.9 3.2 copy-start.1
  9.5 3.5 copy-start.2
  9.5 3.5 copy-start.4
  11.3 256.5 %all-gather.7.cloned.1.call-start = ((), (), s32[]{:S(2)}) async-start(), calls=%async_computation.1 | async-start | bytes 9732096 | tf_op jit(solution)/shard_map/all_gather | solution.py:23
  11.6 256.2 %copy-start.5 = (bf16[768,192]{0,1:T(8,128)(2,1)S(1)}, bf16[768,192]{0,1:T(8,128)(2,1)}, u32[]{:S(2)}) copy-start(bf16[768,192]{0,1:T(8,128)(2,1)} %param.10) | copy-start | bytes 884740
  12.9 363.3 %all-reduce.2.cloned.1.call-start = ((), (), s32[]{:S(2)}) async-start(), calls=%async_computation.4 | async-start | bytes 131072 | tf_op jit(solution)/shard_map/psum | solution.py:41
  14.1 467.9 %all-gather.5.cloned.1.call-start = ((), (), s32[]{:S(2)}) async-start(), calls=%async_computation | async-start | bytes 9732096 | tf_op jit(solution)/shard_map/all_gather | solution.py:31
  14.9 505.6 %all-gather.11.cloned.1.call-start = ((), (), s32[]{:S(2)}) async-start(), calls=%async_computation.3 | async-start | bytes 2654208 | tf_op jit(solution)/shard_map/all_gather | solution.py:28
Sparse Core Ops, SparseCore 0:
  11.5 42.4 all-gather.8
  55.7 212.0 all-gather.6
  270.2 211.7 all-gather.4
  483.7 36.7 all-gather.10
Sparse Core Ops, SparseCore 1:
  18.9 357.3 all-reduce.1
where the time goes:
time: 535 us
  waiting for transfers between devices  498 us (93%)
  matrix products  15.4 us (3%)
  between operations  15.3 us (3%)
    all_gather x1, waiting for transfers between devices, on_device(): lax.all_gather(integrals, 'col', axis=1, tiled=True)  214 us
    all_gather x1, waiting for transfers between devices, on_device(): lax.all_gather(amplitudes, 'col', axis=1, tiled=True)  104 us
    psum x1, waiting for transfers between devices, on_device(): totals = lax.psum(partial_sums, ('row', 'col'))  101 us
    all_gather x1, waiting for transfers between devices, on_device(): amp_columns = lax.all_gather(amplitudes, 'row', axis=0, tiled=True)  39 us
    all_gather x1, waiting for transfers between devices, on_device(): inter_columns = lax.all_gather(intermediate, 'row', axis=0, tiled=True)  38.5 us
  transfers between devices with their start and end apart: 5, of which 5 were waited for; matrix products, arithmetic and copies ran while one was open for 2% of the time, Pallas kernels for 0%

commit v1 on v0

--- a/solution.py
+++ b/solution.py
@@ -38,7 +38,8 @@
     )
     chosen = jnp.dot(selector, pair_amps, preferred_element_type=jnp.float32).astype(jnp.bfloat16)
     partial_sums = jnp.dot(chosen, ladder_ints, preferred_element_type=jnp.float32)
-    totals = lax.psum(partial_sums, ("row", "col"))
+    parts = lax.all_gather(partial_sums, ("row", "col"), axis=0, tiled=False)
+    totals = parts.sum(axis=0)
     share_width = totals.shape[1] // lax.axis_size("col")
     ladder = lax.dynamic_slice_in_dim(totals, lax.axis_index("col") * share_width, share_width, 1)
     return (cycle_residual, ladder)

time: 535 us -> 1270 us (2.37)
  waiting for transfers between devices: 498 us -> 1220 us
    all_gather x0 -> x1, waiting for transfers between devices: none -> 724 us  [on_device(): parts = lax.all_gather(partial_sums, ('row', 'col'), axis=0, tiled=False)]
    psum x1 -> x0, waiting for transfers between devices: 101 us -> none  [on_device(): totals = lax.psum(partial_sums, ('row', 'col'))]
    all_gather x1, waiting for transfers between devices: 104 us -> 206 us  [on_device(): lax.all_gather(amplitudes, 'col', axis=1, tiled=True)]
  transfers between devices with their start and end apart: 5 -> 5, of which waited for: 5 -> 5; matrix products, arithmetic and copies ran while one was open for 2% -> 1% of each run, Pallas kernels for 0% -> 0%
where the time goes in v1:
time: 1270 us; the launch traced here: 1260 us
  waiting for transfers between devices  1220 us (96%)
  matrix products  15.4 us (1%)
  between operations  13.9 us (1%)
    all_gather x1, waiting for transfers between devices, on_device(): parts = lax.all_gather(partial_sums, ('row', 'col'), axis=0, tiled=False)  724 us
    all_gather x1, waiting for transfers between devices, on_device(): lax.all_gather(integrals, 'col', axis=1, tiled=True)  213 us
    all_gather x1, waiting for transfers between devices, on_device(): lax.all_gather(amplitudes, 'col', axis=1, tiled=True)  206 us
    all_gather x1, waiting for transfers between devices, on_device(): amp_columns = lax.all_gather(amplitudes, 'row', axis=0, tiled=True)  40.3 us
    all_gather x1, waiting for transfers between devices, on_device(): inter_columns = lax.all_gather(intermediate, 'row', axis=0, tiled=True)  37.9 us
  transfers between devices with their start and end apart: 5, of which 5 were waited for; matrix products, arithmetic and copies ran while one was open for 1% of the time, Pallas kernels for 0%

profile of v1, /device:TPU:1, one launch (start us, length us, event | category | flops | bytes accessed | tf_op | source)
XLA Modules:
  0.0 1263.3 jit_solution(3291934152193162963)
XLA Ops:
  7.2 0.0 copy-start
  7.2 0.0 all-gather.11.cloned.1.call-start
  7.2 0.8 convert_element_type.17
  8.0 0.2 broadcast_in_dim.4
  8.2 0.4 reshape.14
  8.6 0.0 copy-start.5
  8.7 1.8 mul.12
  10.4 0.0 all-gather.11.cloned.1.call-update
  10.5 0.0 all-gather.9.cloned.1.call-start
  10.5 0.2 broadcast_in_dim.5
  10.7 0.4 reshape.15
  11.2 0.8 mul.14
  11.9 0.0 all-gather.9.cloned.1.call-update
  12.0 0.0 all-gather.7.cloned.1.call-start
  12.0 0.7 all-gather.7.cloned.1.call-update
  12.7 0.0 copy-start.2
  12.7 0.0 copy-start.4
  12.7 0.0 all-gather.13.cloned.1.call-start
  12.8 40.3 %all-gather.11.cloned.1.call-done = bf16[6144,192]{0,1:T(8,128)(2,1)} async-done(((bf16[768,192]{0,1:T(8,128)(2,1)}), bf16[6144,192]{0,1:T(8,128)(2,1)}) %all-gather.11.cloned.1.call-update) | async-done | bytes 2359312 | tf_op jit(solution)/shard_map/all_gather | solution.py:20
  53.1 213.4 %all-gather.9.cloned.1.call-done = bf16[768,6144]{0,1:T(8,128)(2,1)} async-done(((bf16[768,192]{0,1:T(8,128)(2,1)}), bf16[768,6144]{0,1:T(8,128)(2,1)}) %all-gather.9.cloned.1.call-update) | async-done | bytes 9437200 | tf_op jit(solution)/shard_map/all_gather | solution.py:23
  266.4 7.1 fusion
  273.5 0.0 all-gather.13.cloned.1.call-update
  273.6 0.0 all-gather.15.cloned.1.call-start
  273.6 0.0 copy-done
  273.7 1.1 fusion.1
  274.7 0.0 all-gather.15.cloned.1.call-update
  274.8 205.5 %all-gather.7.cloned.1.call-done = bf16[768,6144]{0,1:T(8,128)(2,1)} async-done(((bf16[768,192]{0,1:T(8,128)(2,1)}), bf16[768,6144]{0,1:T(8,128)(2,1)}) %all-gather.7.cloned.1.call-update) | async-done | bytes 9437200 | tf_op jit(solution)/shard_map/all_gather | solution.py:31
  480.3 37.9 %all-gather.13.cloned.1.call-done = bf16[6144,192]{0,1:T(8,128)(2,1)} async-done(((bf16[768,192]{0,1:T(8,128)(2,1)}), bf16[6144,192]{0,1:T(8,128)(2,1)}) %all-gather.13.cloned.1.call-update) | async-done | bytes 2359312 | tf_op jit(solution)/shard_map/all_gather | solution.py:28
  518.2 7.2 fusion.4
  525.4 724.1 %all-gather.15.cloned.1.call-done = f32[4096,1024]{1,0:T(8,128)} async-done(((f32[16,1024]{1,0:T(8,128)}), f32[4096,1024]{1,0:T(8,128)}) %all-gather.15.cloned.1.call-update) | async-done | bytes 16777232 | tf_op jit(solution)/shard_map/all_gather | solution.py:41
  1249.5 6.6 reduce_sum.9
  1256.1 0.7 constant_dynamic-slice_fusion
  (8 shorter events, 0.0 us)
Async XLA Ops:
  7.2 266.5 %copy-start = (bf16[768,1024]{1,0:T(8,128)(2,1)S(1)}, bf16[768,1024]{1,0:T(8,128)(2,1)}, u32[]{:S(2)}) copy-start(bf16[768,1024]{1,0:T(8,128)(2,1)} %param.14) | copy-start | bytes 4718596
  7.2 3.3 copy-start.3
  7.2 45.9 %all-gather.11.cloned.1.call-start = ((), (), s32[]{:S(2)}) async-start(), calls=%async_computation.2 | async-start | bytes 2654208 | tf_op jit(solution)/shard_map/all_gather | solution.py:20
  8.0 3.1 copy-start.1
  8.6 257.8 %copy-start.5 = (bf16[768,192]{0,1:T(8,128)(2,1)S(1)}, bf16[768,192]{0,1:T(8,128)(2,1)}, u32[]{:S(2)}) copy-start(bf16[768,192]{0,1:T(8,128)(2,1)} %param.10) | copy-start | bytes 884740
  10.5 256.0 %all-gather.9.cloned.1.call-start = ((), (), s32[]{:S(2)}) async-start(), calls=%async_computation.1 | async-start | bytes 9732096 | tf_op jit(solution)/shard_map/all_gather | solution.py:23
  12.0 468.3 %all-gather.7.cloned.1.call-start = ((), (), s32[]{:S(2)}) async-start(), calls=%async_computation | async-start | bytes 9732096 | tf_op jit(solution)/shard_map/all_gather | solution.py:31
  12.7 260.9 %copy-start.2 = (bf16[64,768]{1,0:T(8,128)(2,1)S(1)}, bf16[64,768]{1,0:T(8,128)(2,1)}, u32[]{:S(2)}) copy-start(bf16[64,768]{1,0:T(8,128)(2,1)} %param.13) | copy-start | bytes 294916
  12.7 260.9 %copy-start.4 = (s32[16]{0:T(128)S(1)}, s32[16]{0:T(128)}, u32[]{:S(2)}) copy-start(s32[16]{0:T(128)} %param.15) | copy-start | bytes 196
  12.7 505.5 %all-gather.13.cloned.1.call-start = ((), (), s32[]{:S(2)}) async-start(), calls=%async_computation.3 | async-start | bytes 2654208 | tf_op jit(solution)/shard_map/all_gather | solution.py:28
  273.6 975.9 %all-gather.15.cloned.1.call-start = ((), (), s32[]{:S(2)}) async-start(), calls=%async_computation.4 | async-start | bytes 16842752 | tf_op jit(solution)/shard_map/all_gather | solution.py:41
Sparse Core Ops, SparseCore 0:
  10.6 42.4 all-gather.10
  54.9 211.5 all-gather.8
  268.8 211.4 all-gather.6
  482.0 36.1 all-gather.12
  519.9 729.5 all-gather.14

commit v2 on v0

--- a/solution.py
+++ b/solution.py
@@ -2,6 +2,7 @@
 import jax.numpy as jnp
 from jax import lax
 from jax.sharding import PartitionSpec as P
+from jax.lax import all_to_all, axis_size
 
 
 def widen(mask, field):
@@ -19,10 +20,14 @@
     baseline = widen(int_mask, base_ints)
     amp_columns = lax.all_gather(amplitudes, "row", axis=0, tiled=True)
     section = amp_columns
+
+    def pack_joints(u):
+        return jnp.concatenate(
+            all_to_all(jnp.stack(axis_size("col") * [u], axis=0), "col", 0, 0), axis=1
+        )
+
     summed = baseline.astype(jnp.float32) + jnp.dot(
-        lax.all_gather(integrals, "col", axis=1, tiled=True),
-        section,
-        preferred_element_type=jnp.float32,
+        pack_joints(integrals), section, preferred_element_type=jnp.float32
     )
     intermediate = summed.astype(jnp.bfloat16)
     inter_columns = lax.all_gather(intermediate, "row", axis=0, tiled=True)

time: 535 us -> 511 us (0.955)
  waiting for transfers between devices: 498 us -> 461 us
  starting transfers between devices: 0.2 us -> 9.62 us
    all_gather x1 -> x0, waiting for transfers between devices: 214 us -> none  [on_device(): lax.all_gather(integrals, 'col', axis=1, tiled=True)]
    all_to_all x0 -> x1, waiting for transfers between devices: none -> 165 us  [pack_joints(): all_to_all(jnp.stack(axis_size('col') * [u], axis=0), 'col', 0, 0)]
    psum x1, waiting for transfers between devices: 101 us -> 260 us  [on_device(): totals = lax.psum(partial_sums, ('row', 'col'))]
    all_gather x1, waiting for transfers between devices: 104 us -> 0.01 us  [on_device(): lax.all_gather(amplitudes, 'col', axis=1, tiled=True)]
    all_gather x1, waiting for transfers between devices: 38.5 us -> 0.01 us  [on_device(): inter_columns = lax.all_gather(intermediate, 'row', axis=0, tiled=True)]
    all_to_all x0 -> x1, starting transfers between devices: none -> 9.46 us  [pack_joints(): all_to_all(jnp.stack(axis_size('col') * [u], axis=0), 'col', 0, 0)]
  transfers between devices with their start and end apart: 5 -> 5, of which waited for: 5 -> 3; matrix products, arithmetic and copies ran while one was open for 2% -> 3% of each run, Pallas kernels for 0% -> 0%
where the time goes in v2:
time: 511 us
  waiting for transfers between devices  461 us (90%)
  matrix products  15.6 us (3%)
  between operations  15.3 us (3%)
  starting transfers between devices  9.62 us (2%)
  local copies, waits for them, and re-layouts  7.37 us (1%)
    psum x1, waiting for transfers between devices, on_device(): totals = lax.psum(partial_sums, ('row', 'col'))  260 us
    all_to_all x1, waiting for transfers between devices, pack_joints(): all_to_all(jnp.stack(axis_size('col') * [u], axis=0), 'col', 0, 0)  165 us
    all_gather x1, waiting for transfers between devices, on_device(): amp_columns = lax.all_gather(amplitudes, 'row', axis=0, tiled=True)  34.9 us
  transfers between devices with their start and end apart: 5, of which 3 were waited for; matrix products, arithmetic and copies ran while one was open for 3% of the time, Pallas kernels for 0%

profile of v2, /device:TPU:1, one launch (start us, length us, event | category | flops | bytes accessed | tf_op | source)
XLA Modules:
  0.0 511.2 jit_solution(16565238891689289322)
XLA Ops:
  8.0 0.0 copy-start
  8.0 0.0 copy-start.3
  8.0 0.0 all-gather.6.cloned.1.call-start
  8.1 0.8 convert_element_type.17
  8.9 0.2 broadcast_in_dim.4
  9.0 0.4 reshape.22
  9.5 1.7 mul.12
  11.2 0.0 all-gather.6.cloned.1.call-update
  11.2 0.0 copy-done.3
  11.3 0.2 broadcast_in_dim.5
  11.4 0.4 reshape.23
  11.9 0.0 copy-done.1
  11.9 0.1 mul.14
  12.0 4.8 stack.2
  16.8 9.5 %all-to-all-start = ((bf16[32,768,192]{1,2,0:T(8,128)(2,1)}), bf16[32,768,192]{1,2,0:T(8,128)(2,1)}, u32[]{:S(2)}, u32[]{:S(2)}) async-start(bf16[32,768,192]{1,2,0:T(8,128)(2,1)} %stack.2), calls=%async_computation | async-start | bytes 18874368 | tf_op jit(solution)/shard_map/all_to_all | solution.py:26
  26.2 0.0 all-reduce.2.cloned.1.call-start
  26.3 0.0 copy-done
  26.3 0.0 copy-done.2
  26.3 0.0 copy-done.4
  26.3 1.1 fusion.1
  27.4 0.0 all-reduce.2.cloned.1.call-update
  27.4 0.0 all-gather.4.cloned.1.call-start
  27.5 0.7 all-gather.4.cloned.1.call-update
  28.2 0.0 all-gather.8.cloned.1.call-start
  28.2 34.9 %all-gather.6.cloned.1.call-done = bf16[6144,192]{0,1:T(8,128)(2,1)} async-done(((bf16[768,192]{0,1:T(8,128)(2,1)}), bf16[6144,192]{0,1:T(8,128)(2,1)}) %all-gather.6.cloned.1.call-update) | async-done | bytes 2359312 | tf_op jit(solution)/shard_map/all_gather | solution.py:21
  63.1 165.2 %all-to-all-done = bf16[32,768,192]{1,2,0:T(8,128)(2,1)} async-done(((bf16[32,768,192]{1,2,0:T(8,128)(2,1)}), bf16[32,768,192]{1,2,0:T(8,128)(2,1)}, u32[]{:S(2)}, u32[]{:S(2)}) %all-to-all-start) | async-done | bytes 9437216 | tf_op jit(solution)/shard_map/all_to_all | solution.py:26
  228.2 0.0 copy-done.5
  228.2 7.3 %fusion = bf16[768,192]{0,1:T(8,128)(2,1)} fusion(bf16[6144,192]{0,1:T(8,128)(2,1)} %all-gather.6.cloned.1.call-done, bf16[768,6144]{0,1:T(8,128)(2,1)} %bitcast.1, bf16[768,192]{0,1:T(8,128)(2,1)S(1)} %copy-done.5, bf16[768,192]{0,1:T(8,128)(2,1)S(1)} %reshape.23), kind=kOutput, calls=%fused_computation.1 | convolution fusion | flops 1812529152 | bytes 12681216 | tf_op jit(solution)/shard_map/dot_general | solution.py:29
  235.5 0.0 all-gather.8.cloned.1.call-update
  235.6 259.9 %all-reduce.2.cloned.1.call-done = f32[16,1024]{1,0:T(8,128)} async-done(((f32[16,1024]{1,0:T(8,128)}), f32[16,1024]{1,0:T(8,128)}) %all-reduce.2.cloned.1.call-update) | async-done | bytes 65552 | tf_op jit(solution)/shard_map/psum | solution.py:46
  495.5 1.4 constant_dynamic-slice_fusion
  496.9 7.2 %fusion.4 = f32[768,192]{0,1:T(8,128)} fusion(bf16[6144,192]{0,1:T(8,128)(2,1)} %all-gather.8.cloned.1.call-done, bf16[768,6144]{0,1:T(8,128)(2,1)} %all-gather.4.cloned.1.call-done), kind=kOutput, calls=%fused_computation.7 | convolution fusion | flops 1811939328 | bytes 12386304 | tf_op jit(solution)/shard_map/dot_general | solution.py:35
  (7 shorter events, 0.0 us)
Async XLA Ops:
  8.0 18.3 %copy-start = (bf16[768,1024]{1,0:T(8,128)(2,1)S(1)}, bf16[768,1024]{1,0:T(8,128)(2,1)}, u32[]{:S(2)}) copy-start(bf16[768,1024]{1,0:T(8,128)(2,1)} %param.14) | copy-start | bytes 4718596
  8.0 3.2 copy-start.3
  8.0 55.0 %all-gather.6.cloned.1.call-start = ((), (), s32[]{:S(2)}) async-start(), calls=%async_computation.2 | async-start | bytes 2654208 | tf_op jit(solution)/shard_map/all_gather | solution.py:21
  8.9 3.0 copy-start.1
  16.7 9.5 %copy-start.2 = (bf16[64,768]{1,0:T(8,128)(2,1)S(1)}, bf16[64,768]{1,0:T(8,128)(2,1)}, u32[]{:S(2)}) copy-start(bf16[64,768]{1,0:T(8,128)(2,1)} %param.13) | copy-start | bytes 294916
  16.7 9.5 %copy-start.4 = (s32[16]{0:T(128)S(1)}, s32[16]{0:T(128)}, u32[]{:S(2)}) copy-start(s32[16]{0:T(128)} %param.15) | copy-start | bytes 196
  16.7 211.5 %copy-start.5 = (bf16[768,192]{0,1:T(8,128)(2,1)S(1)}, bf16[768,192]{0,1:T(8,128)(2,1)}, u32[]{:S(2)}) copy-start(bf16[768,192]{0,1:T(8,128)(2,1)} %param.10) | copy-start | bytes 884740
  16.8 211.5 %all-to-all-start = ((bf16[32,768,192]{1,2,0:T(8,128)(2,1)}), bf16[32,768,192]{1,2,0:T(8,128)(2,1)}, u32[]{:S(2)}, u32[]{:S(2)}) async-start(bf16[32,768,192]{1,2,0:T(8,128)(2,1)} %stack.2), calls=%async_computation | async-start | bytes 18874368 | tf_op jit(solution)/shard_map/all_to_all | solution.py:26
  26.2 469.3 %all-reduce.2.cloned.1.call-start = ((), (), s32[]{:S(2)}) async-start(), calls=%async_computation.4 | async-start | bytes 131072 | tf_op jit(solution)/shard_map/psum | solution.py:46
  27.4 469.5 %all-gather.4.cloned.1.call-start = ((), (), s32[]{:S(2)}) async-start(), calls=%async_computation.1 | async-start | bytes 9732096 | tf_op jit(solution)/shard_map/all_gather | solution.py:36
  28.2 468.7 %all-gather.8.cloned.1.call-start = ((), (), s32[]{:S(2)}) async-start(), calls=%async_computation.3 | async-start | bytes 2654208 | tf_op jit(solution)/shard_map/all_gather | solution.py:33
Sparse Core Ops, SparseCore 0:
  11.4 51.6 all-gather.5
  65.4 304.0 all-gather.3
  371.4 40.0 all-gather.7
Sparse Core Ops, SparseCore 1:
  32.2 463.2 all-reduce.1
